TPU v7x, 256 devices: a whole 4x4x8 slice. The times are simulated.
256 devices in a mesh: dom: 8 (over y, core), run: 32 (over x, z).
Axes of the slice: x: 4, y: 4, z: 8, core: 2. Of those that a mesh axis runs over, the one named last changes fastest.
Arguments:
- ainv: bfloat16 [1, 512, 2, 256, 256], P(None, ('dom', 'run')), as said below
- coupling: bfloat16 [512, 2, 256, 256], P(('dom', 'run')), as said below
- source: bfloat16 [1, 512, 2, 256, 128], P(None, ('dom', 'run')), may hold values from -0.5 to 0.5
Outputs:
- state: float32 [1, 512, 2, 256, 128], P(None, ('dom', 'run'))
Inputs may be any that keep to these rules, and one draw needn't show every extreme that they name: Every block of ainv and of coupling is upper triangular in the orbital order; the diagonal entries of coupling are 1. Every block of coupling is upper triangular with unit diagonal.
All inputs are finite; a program needn't handle non-finite values.
Results may differ from a plain program's by a relative error of at most 0.0032.
Values sent between devices are 32-bit elements; how exact they have to be, the bound alone decides.
A program may use at most 128 MiB of HBM per device.

v0:
```python
import jax
import jax.numpy as jnp
from jax import lax
from jax.sharding import PartitionSpec as P


def carried_in(shard, axis, combine, identity):
    devices, place = (lax.axis_size(axis), lax.axis_index(axis))
    everything = jax.tree.map(lambda part: lax.all_gather(part, axis), shard)
    start = jax.tree.map(
        lambda part, zero: jnp.broadcast_to(jnp.asarray(zero, part.dtype), part.shape),
        shard,
        identity,
    )

    def step(k, before):
        reached = k < place
        new = combine(before, jax.tree.map(lambda part: part[k], everything))
        return jax.tree.map(lambda a, b: jnp.where(reached, a, b), new, before)

    return lax.fori_loop(0, devices, step, start)


def spread(shard, axis, root):
    mine = lax.axis_index(axis) == root
    return lax.psum(jnp.where(mine, shard, jnp.zeros_like(shard)), axis)


def cprod(left, right):
    hp = lax.Precision.HIGHEST
    real = jnp.einsum(
        "...ij,...jk->...ik", left[..., 0, :, :], right[..., 0, :, :], precision=hp
    ) - jnp.einsum("...ij,...jk->...ik", left[..., 1, :, :], right[..., 1, :, :], precision=hp)
    imag = jnp.einsum(
        "...ij,...jk->...ik", left[..., 0, :, :], right[..., 1, :, :], precision=hp
    ) + jnp.einsum("...ij,...jk->...ik", left[..., 1, :, :], right[..., 0, :, :], precision=hp)
    return jnp.stack([real, imag], axis=-3)


def lowprod(left, right, form):
    real = jnp.einsum(
        form, left[:, :, 0], right[..., 0, :, :], preferred_element_type=jnp.float32
    ) - jnp.einsum(form, left[:, :, 1], right[..., 1, :, :], preferred_element_type=jnp.float32)
    imag = jnp.einsum(
        form, left[:, :, 0], right[..., 1, :, :], preferred_element_type=jnp.float32
    ) + jnp.einsum(form, left[:, :, 1], right[..., 0, :, :], preferred_element_type=jnp.float32)
    return jnp.stack([real, imag], axis=2)


def compose(earlier, later):
    return (cprod(later[0], earlier[0]), cprod(later[0], earlier[1]) + later[1])


def shards(ainv, coupling, source):
    energies = ainv.shape[0]
    slab_count = ainv.shape[1]
    orbitals = ainv.shape[3]
    columns = source.shape[4]
    hops = -lowprod(ainv, coupling, "esij,sjk->esik")
    hops = lax.optimization_barrier(hops.astype(jnp.bfloat16)).astype(jnp.float32)
    injects = lowprod(ainv, source, "esij,esjk->esik")
    own_map = hops[:, 0]
    own_off = injects[:, 0]
    slab = 1
    own_off = cprod(hops[:, slab], own_off) + injects[:, slab]
    own_map = cprod(hops[:, slab], own_map)
    eye = jnp.eye(orbitals, dtype=jnp.float32)
    unit = jnp.broadcast_to(
        jnp.stack([eye, jnp.zeros_like(eye)], axis=0), (energies, 2, orbitals, orbitals)
    )
    nothing = jnp.zeros((energies, 2, orbitals, columns), jnp.float32)
    before = carried_in((own_map, own_off), "run", compose, (unit, nothing))
    through = compose(before, (own_map, own_off))
    whole = (
        spread(through[0], "run", lax.axis_size("run") - 1),
        spread(through[1], "run", lax.axis_size("run") - 1),
    )
    earlier = carried_in((whole[0], whole[1]), "dom", compose, (unit, nothing))
    arriving = earlier[1]
    entry = cprod(before[0], arriving) + before[1]
    current = entry
    results = []
    for slab in range(slab_count):
        current = cprod(hops[:, slab], current) + injects[:, slab]
        results.append(current)
    return jnp.stack(results, axis=1)


def solution(mesh):
    in_specs = (
        P(None, ("dom", "run"), None, None, None),
        P(("dom", "run"), None, None, None),
        P(None, ("dom", "run"), None, None, None),
    )
    out_specs = P(None, ("dom", "run"), None, None, None)
    return jax.shard_map(shards, mesh=mesh, in_specs=in_specs, out_specs=out_specs, check_vma=False)
```

profile of v0, /device:TPU:122, one launch (start us, length us, event | category | flops | bytes accessed | tf_op | source)
XLA Modules:
  0.0 685.3 jit_solution(12421350015766170829)
XLA Ops:
  6.5 1.4 fusion.40
  7.9 1.3 fusion.44
  9.2 1.2 fusion.50
  10.4 1.2 fusion.52
  11.6 1.3 fusion.22
  13.0 1.3 fusion.23
  19.6 95.8 %all-gather.6.cloned.1.call-done = f32[32,1,2,256,128]{4,3,2,1,0:T(8,128)} async-done(((f32[1,1,2,256,128]{4,3,2,1,0:T(8,128)}), f32[32,1,2,256,128]{4,3,2,1,0:T(8,128)}) %all-gather.6.cloned.1.call-update) | async-done | bytes 8388624 | tf_op jit(solution)/shard_map/all_gather | solution.py:9
  115.3 139.4 %all-gather.12.cloned.1.call-done = f32[32,2,256,256]{3,2,1,0:T(8,128)} async-done(((f32[1,2,256,256]{3,2,1,0:T(8,128)}), f32[32,2,256,256]{3,2,1,0:T(8,128)}) %all-gather.12.cloned.1.call-update) | async-done | bytes 16777232 | tf_op jit(solution)/shard_map/all_gather | solution.py:9
  254.7 173.0 %while.30 = (s32[]{:T(128)}, f32[1,2,256,256]{3,2,1,0:T(8,128)S(1)}, f32[1,2,256,128]{3,2,1,0:T(8,128)S(1)}, s32[]{:T(128)}, f32[32,1,2,256,256]{4,3,2,1,0:T(8,1...) while((s32[]{:T(128)}, f32[1,2,256,256]{3,2,1,0:T(8,128)S(1)}, ...), condition=%wide.region_1.2_spmd.clone, body=%wide.region_0.1_spmd.clone.sunk | while | flops 1208745984 | bytes 10223731 | solution.py:21
  254.7 1.1 dynamic-slice_bitcast_fusion.4
  257.4 1.0 fusion.161
  260.1 1.1 dynamic-slice_bitcast_fusion.4
  262.8 1.0 fusion.161
  265.5 1.1 dynamic-slice_bitcast_fusion.4
  268.2 1.0 fusion.161
  270.9 1.1 dynamic-slice_bitcast_fusion.4
  273.6 1.0 fusion.161
  276.3 1.1 dynamic-slice_bitcast_fusion.4
  279.0 1.0 fusion.161
  281.7 1.1 dynamic-slice_bitcast_fusion.4
  284.4 1.0 fusion.161
  287.1 1.1 dynamic-slice_bitcast_fusion.4
  289.8 1.0 fusion.161
  292.5 1.1 dynamic-slice_bitcast_fusion.4
  295.2 1.0 fusion.161
  297.9 1.1 dynamic-slice_bitcast_fusion.4
  303.4 1.1 dynamic-slice_bitcast_fusion.4
  308.8 1.1 dynamic-slice_bitcast_fusion.4
  314.2 1.1 dynamic-slice_bitcast_fusion.4
  319.6 1.1 dynamic-slice_bitcast_fusion.4
  325.0 1.1 dynamic-slice_bitcast_fusion.4
  330.4 1.1 dynamic-slice_bitcast_fusion.4
  335.8 1.1 dynamic-slice_bitcast_fusion.4
  341.2 1.1 dynamic-slice_bitcast_fusion.4
  343.9 1.0 fusion.161
  346.6 1.1 dynamic-slice_bitcast_fusion.4
  352.0 1.1 dynamic-slice_bitcast_fusion.4
  357.4 1.1 dynamic-slice_bitcast_fusion.4
  362.8 1.1 dynamic-slice_bitcast_fusion.4
  368.2 1.1 dynamic-slice_bitcast_fusion.4
  373.6 1.1 dynamic-slice_bitcast_fusion.4
  379.0 1.1 dynamic-slice_bitcast_fusion.4
  384.4 1.1 dynamic-slice_bitcast_fusion.4
  389.9 1.1 dynamic-slice_bitcast_fusion.4
  395.3 1.1 dynamic-slice_bitcast_fusion.4
  400.7 1.1 dynamic-slice_bitcast_fusion.4
  406.1 1.1 dynamic-slice_bitcast_fusion.4
  411.5 1.1 dynamic-slice_bitcast_fusion.4
  416.9 1.1 dynamic-slice_bitcast_fusion.4
  422.3 1.1 dynamic-slice_bitcast_fusion.4
  431.6 1.6 fusion.38
  433.3 146.6 %all-reduce.4.cloned.1.call-done = (f32[1,1,2,256,256]{4,3,2,1,0:T(8,128)}, f32[1,1,2,256,128]{4,3,2,1,0:T(8,128)}) async-done(((f32[1,1,2,256,256]{4,3,2,1,0:T(8,128)}, f32[1,1,2,256,128]{4,3,2,1,0:T(8,128)}), (f32[1,1,2,256,256]{4,3,2,1,0:T(8,128)}, f32[1,1,2,256,128]{4,3,2,1,0:T(8,128)})) %all-reduce.4.cloned.1.call-update) | async-done | bytes 786448 | tf_op jit(solution)/shard_map/psum | solution.py:26
  580.6 27.4 %all-gather.10.cloned.1.call-done = f32[8,1,2,256,128]{4,3,2,1,0:T(8,128)} async-done(((f32[1,1,2,256,128]{4,3,2,1,0:T(8,128)}), f32[8,1,2,256,128]{4,3,2,1,0:T(8,128)}) %all-gather.10.cloned.1.call-update) | async-done | bytes 2097168 | tf_op jit(solution)/shard_map/all_gather | solution.py:9
  608.0 36.1 %all-gather.8.cloned.1.call-done = f32[8,1,2,256,256]{4,3,2,1,0:T(8,128)} async-done(((f32[1,1,2,256,256]{4,3,2,1,0:T(8,128)}), f32[8,1,2,256,256]{4,3,2,1,0:T(8,128)}) %all-gather.8.cloned.1.call-update) | async-done | bytes 4194320 | tf_op jit(solution)/shard_map/all_gather | solution.py:9
  644.1 29.7 %while.31 = (s32[]{:T(128)}, f32[1,2,256,128]{3,2,1,0:T(8,128)S(1)}, s32[]{:T(128)}, f32[8,1,2,256,256]{4,3,2,1,0:T(8,128)}, f32[8,1,2,256,128]{4,3,2,1,0:T(8,128)}, /*index=5*/s32[]{:T(128)}, s32[]{:T(128)}) while((s32[]{:T(128)}, f32[1,2,256,128]{3,2,1,0:T(8,128)S(1)}, s32[]{:T(128)}, f32[8,1,2,256,256]{4,3,2,1,0:T(8,128)}, ...), condition=%wide.region_5.6_spmd.clone, body=%wide.region_4.5_spmd.clone.sunk | while | flops 403046400 | bytes 4980842 | solution.py:21
  644.1 1.1 dynamic-slice_bitcast_fusion.5
  647.8 1.1 dynamic-slice_bitcast_fusion.5
  651.5 1.1 dynamic-slice_bitcast_fusion.5
  655.2 1.1 dynamic-slice_bitcast_fusion.5
  658.9 1.1 dynamic-slice_bitcast_fusion.5
  661.6 1.0 fusion.166
  662.6 1.1 dynamic-slice_bitcast_fusion.5
  666.4 1.1 dynamic-slice_bitcast_fusion.5
  670.1 1.1 dynamic-slice_bitcast_fusion.5
  (451 shorter events, 159.8 us)
Async XLA Ops:
  6.5 7.9 %copy-start = (bf16[1,2,2,256,256]{4,3,2,1,0:T(8,128)(2,1)S(1)}, bf16[1,2,2,256,256]{4,3,2,1,0:T(8,128)(2,1)}, u32[]{:S(2)}) copy-start(bf16[1,2,2,256,256]{4,3,2,1,0:T(8,128)(2,1)} %param.7) | copy-start | bytes 1572868
  6.5 7.9 %copy-start.2 = (bf16[1,2,2,256,128]{4,3,2,1,0:T(8,128)(2,1)S(1)}, bf16[1,2,2,256,128]{4,3,2,1,0:T(8,128)(2,1)}, u32[]{:S(2)}) copy-start(bf16[1,2,2,256,128]{4,3,2,1,0:T(8,128)(2,1)} %param.9) | copy-start | bytes 786436
  6.5 108.8 %all-gather.6.cloned.1.call-start = ((), (), s32[]{:S(2)}) async-start(), calls=%async_computation | async-start | bytes 8650752 | tf_op jit(solution)/shard_map/all_gather | solution.py:9
  16.2 0.6 copy-start.1
  17.6 237.1 %all-gather.12.cloned.1.call-start = ((), (), s32[]{:S(2)}) async-start(), calls=%async_computation.3 | async-start | bytes 17301504 | tf_op jit(solution)/shard_map/all_gather | solution.py:9
  19.4 560.5 %all-reduce.4.cloned.1.call-start = ((), (), s32[]{:S(2)}) async-start(), calls=%async_computation.4 | async-start | bytes 1572864 | tf_op jit(solution)/shard_map/psum | solution.py:26
  433.3 174.7 %all-gather.10.cloned.1.call-start = ((), (), s32[]{:S(2)}) async-start(), calls=%async_computation.2 | async-start | bytes 2359296 | tf_op jit(solution)/shard_map/all_gather | solution.py:9
  580.0 64.1 %all-gather.8.cloned.1.call-start = ((), (), s32[]{:S(2)}) async-start(), calls=%async_computation.1 | async-start | bytes 4718592 | tf_op jit(solution)/shard_map/all_gather | solution.py:9
Sparse Core Ops, SparseCore 0:
  17.7 97.5 all-gather.5
  117.9 136.7 all-gather.11
  433.4 146.5 all-reduce.3
  581.7 26.2 all-gather.9
  609.7 34.3 all-gather.7
where the time goes:
time: 693 us; the launch traced here: 685 us
  waiting for transfers between devices  446 us (64%)
  matrix products  126 us (18%)
  other arithmetic  50.9 us (7%)
  local copies, waits for them, and re-layouts  44.7 us (6%)
  between operations  13.5 us (2%)
    all_gather x4, waiting for transfers between devices, carried_in(): everything = jax.tree.map(lambda part: lax.all_gather(part, axis), shard)  299 us
    psum x1, waiting for transfers between devices, spread(): return lax.psum(jnp.where(mine, shard, jnp.zeros_like(shard)), axis)  147 us
    select_n x72, other arithmetic, step(): return jax.tree.map(lambda a, b: jnp.where(reached, a, b), new, before)  45.7 us
    squeeze x40, local copies, waits for them, and re-layouts, step(): new = combine(before, jax.tree.map(lambda part: part[k], everything))  43.2 us
    dot_general x79, matrix products, cprod(): jnp.einsum('...ij,...jk->...ik', left[..., 1, :, :], right[..., 1, :, :],...  29.6 us
    dot_general x79, matrix products, cprod(): jnp.einsum('...ij,...jk->...ik', left[..., 0, :, :], right[..., 0, :, :],...  29.5 us
    dot_general x79, matrix products, cprod(): jnp.einsum('...ij,...jk->...ik', left[..., 1, :, :], right[..., 0, :, :],...  29.5 us
    dot_general x79, matrix products, cprod(): jnp.einsum('...ij,...jk->...ik', left[..., 0, :, :], right[..., 1, :, :],...  29.5 us
  transfers between devices with their start and end apart: 5, of which 5 were waited for; matrix products, arithmetic and copies ran while one was open for 0% of the time, Pallas kernels for 0%

commit v1 on v0

v1 whole, which is shorter than its diff:
```python
import jax
import jax.numpy as jnp
from jax import lax
from jax.experimental import pallas as pl
from jax.experimental.pallas import tpu as pltpu
from jax.sharding import PartitionSpec as P

MESH = pl.DeviceIdType.MESH
F32 = jnp.float32
BF16 = jnp.bfloat16

NX = 4
H = 128
R = 32
NA2 = H // R
NA11 = H // 2 // R
NB = H // R
A11_ROW = H
B_ROW = H + H // 2
ROWS = B_ROW + H
A11_CH = NA2
B_CH = NA2 + NA11
NC = B_CH + NB


def dot(a, b):
    return lax.dot_general(a, b, (((1,), (0,)), ((), ())), preferred_element_type=F32)


def split(x):
    hi = x.astype(BF16)
    return hi, (x - hi.astype(F32)).astype(BF16)


def rows(start, size):
    return pl.ds(pl.multiple_of(start, 8), size)


def put_tile(w, t, top):
    w[t, 0:H, :] = top
    w[t, H : 2 * H, 0:H] = -top[:, H:]
    w[t, H : 2 * H, H:] = top[:, :H]


def put_weights(w, buf):
    def one(t, top):
        hi, lo = split(top)
        put_tile(w.at[0], t, hi)
        put_tile(w.at[1], t, lo)

    a11 = buf[A11_ROW : A11_ROW + H // 2, :]
    one(0, jnp.concatenate([a11[:, : 2 * H], a11[:, 2 * H :]], axis=0))
    one(1, buf[0:H, 0 : 2 * H])
    one(2, buf[0:H, 2 * H :])


def mul3(x, w, t):
    n = x.shape[0]
    hi, lo = split(x)
    both = dot(jnp.concatenate([hi, lo], axis=0), w[0, t])
    return both[:n] + both[n:] + dot(hi, w[1, t])


def mul2(x, w, t):
    n = x.shape[0]
    hi, lo = split(x)
    both = dot(jnp.concatenate([hi, lo], axis=0), w[t])
    return both[:n] + both[n:]


def full(x, w, mul):
    x1, x2 = x[:, : 2 * H], x[:, 2 * H :]
    return jnp.concatenate([mul(x1, w, 0) + mul(x2, w, 1), mul(x2, w, 2)], axis=1)


def kernel(
    ndom, nx, nz, ainv, coup, src, out,
    loc, ez, oz, ex, ox, ed, od, sd, sx, wm, we, wt, wex, wd, wh, inj, fin,
    zs, zr, xs, xr, ds, dr, xds, xdr, zds, zdr,
):
    dom, run = lax.axis_index("dom"), lax.axis_index("run")
    x, z = run // nz, run % nz
    last_z, last_x = z == nz - 1, x == nx - 1

    def at(d, xx, zz):
        return (d, xx * nz + zz)

    z_up, z_dn = at(dom, x, (z + 1) % nz), at(dom, x, (z + nz - 1) % nz)
    x_up, x_dn = at(dom, (x + 1) % nx, z), at(dom, (x + nx - 1) % nx, z)
    d_up, d_dn = at((dom + 1) % ndom, x, z), at((dom + ndom - 1) % ndom, x, z)

    barrier = pltpu.get_barrier_semaphore()
    for who in (z_up, z_dn, x_up, x_dn, d_up, d_dn):
        pl.semaphore_signal(barrier, inc=1, device_id=who, device_id_type=MESH)

    for s in range(2):
        ar, ai = ainv[0, s, 0], ainv[0, s, 1]
        cr, ci = coup[s, 0], coup[s, 1]
        hr = (dot(ai, ci) - dot(ar, cr)).astype(BF16).astype(F32)
        hi = (-(dot(ar, ci) + dot(ai, cr))).astype(BF16).astype(F32)
        for t, (i, j) in enumerate(((0, 0), (0, H), (H, H))):
            top = jnp.concatenate(
                [hr[i : i + H, j : j + H].T, hi[i : i + H, j : j + H].T], axis=1
            )
            put_tile(wh.at[s], t, top.astype(BF16))
        sr, si = src[0, s, 0], src[0, s, 1]
        pr = dot(ar, sr) - dot(ai, si)
        pi = dot(ar, si) + dot(ai, sr)
        for h in range(2):
            inj[s, :, 2 * h * H : (2 * h + 1) * H] = pr[h * H : (h + 1) * H].T
            inj[s, :, (2 * h + 1) * H : (2 * h + 2) * H] = pi[h * H : (h + 1) * H].T
    w1 = wh.at[1]
    a11 = dot(wh[0, 0, 0:H, :], w1[0])
    loc[A11_ROW : A11_ROW + H // 2, : 2 * H] = a11[: H // 2]
    loc[A11_ROW : A11_ROW + H // 2, 2 * H :] = a11[H // 2 :]
    x1, x2 = wh[0, 1, 0:H, :], wh[0, 2, 0:H, :]
    loc[0:H, : 2 * H] = dot(x1, w1[0]) + dot(x2, w1[1])
    loc[0:H, 2 * H :] = dot(x2, w1[2])
    loc[B_ROW:, :] = full(inj[0], w1, mul2) + inj[1]
    put_weights(wm, loc)

    pl.semaphore_wait(barrier, 6)

    def copy(src_ref, dst_ref, c, ssem, rsem, who, first=0):
        r = rows(c * R, R)
        rd = rows((c - first) * R, R)
        return pltpu.make_async_remote_copy(
            src_ref=src_ref.at[r], dst_ref=dst_ref.at[rd], send_sem=ssem, recv_sem=rsem,
            device_id=who, device_id_type=MESH,
        )

    def arrive(buf, rsem, c):
        r = rows(c * R, R)
        pltpu.make_async_remote_copy(
            src_ref=buf.at[r], dst_ref=buf.at[r], send_sem=zs.at[c], recv_sem=rsem.at[c],
            device_id=z_up, device_id_type=MESH,
        ).wait_recv()

    def each(lo, hi, body):
        def step(c, carry):
            body(c)
            return carry

        lax.fori_loop(lo, hi, step, 0)

    def chain(inp, outp, w, own_b, rsem, send, between):
        def a2(c):
            arrive(inp, rsem, c)
            outp[rows(c * R, R), :] = full(inp[rows(c * R, R), :], w, mul3)
            send(c)

        def a11_(c):
            arrive(inp, rsem, c)
            v = inp[rows(c * R, R), :]
            y = mul3(jnp.concatenate([v[:, : 2 * H], v[:, 2 * H :]], axis=0), w, 0)
            outp[rows(c * R, R), :] = jnp.concatenate([y[:R], y[R:]], axis=1)
            send(c)

        def bb(c):
            arrive(inp, rsem, c)
            r = rows(c * R, R)
            outp[r, :] = full(inp[r, :], w, mul3) + own_b[r, :]
            send(c)

        each(0, NA2, a2)
        each(A11_CH, B_CH, a11_)
        between()
        each(B_CH, NC, bb)

    def z_copy(c, src_ref):
        return copy(src_ref, ez, c, zs.at[c], zr.at[c], z_up)

    def zx_copy(c, src_ref):
        return copy(src_ref, ex, c, zs.at[c], xr.at[c], x_up)

    @pl.when(z == 0)
    def _():
        each(0, NC, lambda c: z_copy(c, loc).start())

    @pl.when(z > 0)
    def _():
        def send(c):
            @pl.when(jnp.logical_not(last_z))
            def _():
                z_copy(c, oz).start()

            @pl.when(jnp.logical_and(last_z, x == 0))
            def _():
                zx_copy(c, oz).start()

        def between():
            @pl.when(last_z)
            def _():
                put_weights(wt, oz)

        chain(ez, oz, wm, loc, zr, send, between)
        put_weights(we, ez)

    def x_copy(c):
        return copy(ox, ex, c, xs.at[c], xr.at[c], x_up)

    def xd_copy(c):
        return copy(ox, ed, c, xs.at[c], dr.at[c - B_CH], d_up, first=B_CH)

    first_out = jnp.logical_and(last_x, dom == 0)

    @pl.when(jnp.logical_and(last_z, x > 0))
    def _():
        def send(c):
            @pl.when(jnp.logical_not(last_x))
            def _():
                x_copy(c).start()

            @pl.when(jnp.logical_and(first_out, c >= B_CH))
            def _():
                xd_copy(c).start()

        def between():
            @pl.when(last_x)
            def _():
                put_weights(wd, ox)

        chain(ex, ox, wt, oz, xr, send, between)
        put_weights(wex, ex)

    def d_copy(c):
        return copy(od, ed, c, ds.at[c], dr.at[c], d_up)

    def spread(n, place, buf, ssem, rsem, up, dn):
        plus = (n - 1) // 2

        def up_copy(c):
            return copy(buf, buf, c, ssem.at[0, c], rsem.at[c], up)

        def dn_copy(c):
            return copy(buf, buf, c, ssem.at[1, c], rsem.at[c], dn)

        to_up = jnp.logical_or(place == n - 1, place < plus - 1) if plus else place < 0
        to_dn = place > plus

        def go(c, wait):
            @pl.when(to_up)
            def _():
                cp = up_copy(c)
                cp.wait_send() if wait else cp.start()

            @pl.when(to_dn)
            def _():
                cp = dn_copy(c)
                cp.wait_send() if wait else cp.start()

        return go

    x_go = spread(nx, x, sd, xds, xdr, x_up, x_dn)
    z_go = spread(nz, z, sx, zds, zdr, z_up, z_dn)

    @pl.when(jnp.logical_and(last_z, last_x))
    def _():
        @pl.when(dom == 0)
        def _():
            sd[...] = jnp.zeros_like(sd)

        def step(c):
            r = rows(c * R, R)

            @pl.when(dom > 0)
            def _():
                arrive(ed, dr, c)

                @pl.when(dom < ndom - 1)
                def _():
                    od[r, :] = full(ed[r, :], wd, mul3) + ox[rows(B_ROW + c * R, R), :]
                    d_copy(c).start()

                sd[r, :] = ed[r, :]

            x_go(c, False)

        each(0, NB, step)

    @pl.when(last_z)
    def _():
        def step(c):
            r = rows(c * R, R)

            @pl.when(jnp.logical_not(last_x))
            def _():
                arrive(sd, xdr, c)
                x_go(c, False)

            @pl.when(x == 0)
            def _():
                sx[r, :] = sd[r, :]

            @pl.when(x > 0)
            def _():
                sx[r, :] = full(sd[r, :], wex, mul3) + ex[rows(B_ROW + c * R, R), :]

            z_go(c, False)

        each(0, NB, step)

    def finish(c):
        r = rows(c * R, R)

        @pl.when(jnp.logical_not(last_z))
        def _():
            arrive(sx, zdr, c)
            z_go(c, False)

        @pl.when(z == 0)
        def _():
            fin[0, r, :] = sx[r, :]

        @pl.when(z > 0)
        def _():
            fin[0, r, :] = full(sx[r, :], we, mul3) + ez[rows(B_ROW + c * R, R), :]

        s0 = full(fin[0, r, :], wh.at[0], mul2) + inj[0, r, :]
        fin[0, r, :] = s0
        fin[1, r, :] = full(s0, wh.at[1], mul2) + inj[1, r, :]

    each(0, NB, finish)
    for s in range(2):
        for p in range(2):
            for h in range(2):
                k = (2 * h + p) * H
                out[0, s, p, h * H : (h + 1) * H, :] = fin[s, :, k : k + H].T

    @pl.when(z == 0)
    def _():
        each(0, NC, lambda c: z_copy(c, loc).wait_send())

    @pl.when(jnp.logical_and(z > 0, jnp.logical_not(last_z)))
    def _():
        each(0, NC, lambda c: z_copy(c, oz).wait_send())

    @pl.when(jnp.logical_and(last_z, x == 0))
    def _():
        each(0, NC, lambda c: zx_copy(c, oz).wait_send())

    @pl.when(jnp.logical_and(last_z, jnp.logical_and(x > 0, jnp.logical_not(last_x))))
    def _():
        each(0, NC, lambda c: x_copy(c).wait_send())

    @pl.when(jnp.logical_and(last_z, first_out))
    def _():
        each(B_CH, NC, lambda c: xd_copy(c).wait_send())

    @pl.when(jnp.logical_and(last_z, last_x))
    def _():
        @pl.when(jnp.logical_and(dom > 0, dom < ndom - 1))
        def _():
            each(0, NB, lambda c: d_copy(c).wait_send())

    @pl.when(last_z)
    def _():
        each(0, NB, lambda c: x_go(c, True))

    each(0, NB, lambda c: z_go(c, True))


def build(mesh, nx):
    ndom, nrun = mesh.shape["dom"], mesh.shape["run"]
    nz = nrun // nx

    def shards(ainv, coupling, source):
        big = pltpu.VMEM((ROWS, 4 * H), F32)
        half = pltpu.VMEM((H, 4 * H), F32)
        weights = pltpu.VMEM((2, 3, 2 * H, 2 * H), BF16)
        sem = pltpu.SemaphoreType.DMA

        def body(*refs):
            kernel(ndom, nx, nz, *refs)

        vm = pl.BlockSpec(memory_space=pltpu.VMEM)
        return pl.pallas_call(
            body,
            out_shape=jax.ShapeDtypeStruct(source.shape, F32),
            in_specs=[vm] * 3,
            out_specs=vm,
            scratch_shapes=[
                big, big, big, big, big,
                half, half, half, half,
                weights, weights, weights, weights, weights,
                pltpu.VMEM((2, 3, 2 * H, 2 * H), BF16),
                pltpu.VMEM((2, H, 4 * H), F32),
                pltpu.VMEM((2, H, 4 * H), F32),
                sem((NC,)), sem((NC,)), sem((NC,)), sem((NC,)), sem((NB,)), sem((NB,)),
                sem((2, NB)), sem((NB,)), sem((2, NB)), sem((NB,)),
            ],
            compiler_params=pltpu.CompilerParams(
                collective_id=0, has_side_effects=True, vmem_limit_bytes=48 * 1024 * 1024
            ),
            name="sweep",
        )(ainv, coupling, source)

    in_specs = (
        P(None, ("dom", "run"), None, None, None),
        P(("dom", "run"), None, None, None),
        P(None, ("dom", "run"), None, None, None),
    )
    out_specs = P(None, ("dom", "run"), None, None, None)
    return jax.shard_map(shards, mesh=mesh, in_specs=in_specs, out_specs=out_specs, check_vma=False)


def solution(mesh):
    return build(mesh, NX)
```

time: 693 us -> 99.7 us (0.14); the launches traced: 685 us -> 99.5 us
  waiting for transfers between devices: 446 us -> 0 us
  matrix products: 126 us -> 0 us
  Pallas kernels: 0 us -> 95.6 us
  other arithmetic: 50.9 us -> 0 us
  local copies, waits for them, and re-layouts: 44.7 us -> 3.83 us
  between operations: 13.5 us -> 0.01 us
    all_gather x4 -> x0, waiting for transfers between devices: 299 us -> none  [carried_in(): everything = jax.tree.map(lambda part: lax.all_gather(part, axis), shard)]
    psum x1 -> x0, waiting for transfers between devices: 147 us -> none  [spread(): return lax.psum(jnp.where(mine, shard, jnp.zeros_like(shard)), axis)]
    dot_general x324 -> x0, matrix products: 126 us -> none  [the longest x79 29.6 us: cprod(): jnp.einsum('...ij,...jk->...ik', left[..., 1, :, :], right[..., 1, :, :],...]
    pallas_call x0 -> x1, Pallas kernels: none -> 95.6 us  [shards(): pl.pallas_call(body, out_shape=jax.ShapeDtypeStruct(source.shape, F32), i...]
    select_n x72 -> x0, other arithmetic: 45.7 us -> none  [step(): return jax.tree.map(lambda a, b: jnp.where(reached, a, b), new, before)]
    squeeze x41 -> x0, local copies, waits for them, and re-layouts: 43.3 us -> none  [the longest x40 43.2 us: step(): new = combine(before, jax.tree.map(lambda part: part[k], everything))]
  transfers between devices with their start and end apart: 5 -> 0, of which waited for: 5 -> 0; matrix products, arithmetic and copies ran while one was open for 0% -> 0% of each run, Pallas kernels for 0% -> 0%
where the time goes in v1:
time: 99.7 us; the launch traced here: 99.5 us
  Pallas kernels  95.6 us (96%)
  local copies, waits for them, and re-layouts  3.83 us (4%)
    pallas_call x1, Pallas kernels, shards(): pl.pallas_call(body, out_shape=jax.ShapeDtypeStruct(source.shape, F32), i...  95.6 us
    unnamed x7, local copies, waits for them, and re-layouts  3.83 us

profile of v1, /device:TPU:122, one launch (start us, length us, event | category | flops | bytes accessed | tf_op | source)
XLA Modules:
  0.0 99.5 jit_solution(4360919940067824743)
XLA Ops:
  0.0 0.0 copy-start
  0.0 1.0 %copy-done = bf16[1,2,2,256,256]{4,3,2,1,0:T(8,128)(2,1)S(1)} copy-done((bf16[1,2,2,256,256]{4,3,2,1,0:T(8,128)(2,1)S(1)}, bf16[1,2,2,256,256]{4,3,2,1,0:T(8,128)(2,1)}, u32[]{:S(2)}) %copy-start) | copy-done | bytes 524312
  1.0 0.0 copy-start.1
  1.0 1.0 %copy-done.1 = bf16[2,2,256,256]{3,2,1,0:T(8,128)(2,1)S(1)} copy-done((bf16[2,2,256,256]{3,2,1,0:T(8,128)(2,1)S(1)}, bf16[2,2,256,256]{3,2,1,0:T(8,128)(2,1)}, u32[]{:S(2)}) %copy-start.1) | copy-done | bytes 524312
  2.1 0.0 copy-start.2
  2.1 0.9 copy-done.2
  3.0 95.6 %sweep.1 = f32[1,2,2,256,128]{4,3,2,1,0:T(8,128)S(1)} custom-call(bf16[1,2,2,256,256]{4,3,2,1,0:T(8,128)(2,1)S(1)} %copy-done, bf16[2,2,256,256]{3,2,1,0:T(8,128)(2,1)S(1)} %copy-done.1, bf16[1,2,2,256,128]{4,3,2,1,0:T(8,128)(2,1)S(1)} %copy-done.2), custom_call_target="tpu_custom_call" | custom-call | tf_op jit(solution)/shard_map/sweep/pallas_call | solution.py:377
  98.7 0.8 copy.5
Async XLA Ops:
  0.0 1.0 %copy-start = (bf16[1,2,2,256,256]{4,3,2,1,0:T(8,128)(2,1)S(1)}, bf16[1,2,2,256,256]{4,3,2,1,0:T(8,128)(2,1)}, u32[]{:S(2)}) copy-start(bf16[1,2,2,256,256]{4,3,2,1,0:T(8,128)(2,1)} %refs_0_.1) | copy-start | bytes 1572868
  1.0 1.0 %copy-start.1 = (bf16[2,2,256,256]{3,2,1,0:T(8,128)(2,1)S(1)}, bf16[2,2,256,256]{3,2,1,0:T(8,128)(2,1)}, u32[]{:S(2)}) copy-start(bf16[2,2,256,256]{3,2,1,0:T(8,128)(2,1)} %refs_1_.1) | copy-start | bytes 1572868
  2.1 0.9 copy-start.2

commit v2 on v1

--- a/solution.py
+++ b/solution.py
@@ -11,7 +11,7 @@
 
 NX = 4
 H = 128
-R = 32
+R = 16
 NA2 = H // R
 NA11 = H // 2 // R
 NB = H // R
@@ -74,10 +74,19 @@
 
 
 def kernel(
-    ndom, nx, nz, ainv, coup, src, out,
-    loc, ez, oz, ex, ox, ed, od, sd, sx, wm, we, wt, wex, wd, wh, inj, fin,
+    ndom, nx, nz, ainv_in, coup_in, src_in, out,
+    ainv, coup, src, in_sem, loc, ez, oz, ex, ox, ed, od, sd, sx, wm, we, wt, wex, wd, wh, inj, fin,
     zs, zr, xs, xr, ds, dr, xds, xdr, zds, zdr,
 ):
+    loads = []
+    for s in range(2):
+        loads.append([
+            pltpu.make_async_copy(ainv_in.at[0, s], ainv.at[s], in_sem.at[s, 0]),
+            pltpu.make_async_copy(coup_in.at[s], coup.at[s], in_sem.at[s, 1]),
+            pltpu.make_async_copy(src_in.at[0, s], src.at[s], in_sem.at[s, 2]),
+        ])
+        for load in loads[s]:
+            load.start()
     dom, run = lax.axis_index("dom"), lax.axis_index("run")
     x, z = run // nz, run % nz
     last_z, last_x = z == nz - 1, x == nx - 1
@@ -94,7 +103,9 @@
         pl.semaphore_signal(barrier, inc=1, device_id=who, device_id_type=MESH)
 
     for s in range(2):
-        ar, ai = ainv[0, s, 0], ainv[0, s, 1]
+        for load in loads[s]:
+            load.wait()
+        ar, ai = ainv[s, 0], ainv[s, 1]
         cr, ci = coup[s, 0], coup[s, 1]
         hr = (dot(ai, ci) - dot(ar, cr)).astype(BF16).astype(F32)
         hi = (-(dot(ar, ci) + dot(ai, cr))).astype(BF16).astype(F32)
@@ -103,7 +114,7 @@
                 [hr[i : i + H, j : j + H].T, hi[i : i + H, j : j + H].T], axis=1
             )
             put_tile(wh.at[s], t, top.astype(BF16))
-        sr, si = src[0, s, 0], src[0, s, 1]
+        sr, si = src[s, 0], src[s, 1]
         pr = dot(ar, sr) - dot(ai, si)
         pi = dot(ar, si) + dot(ai, sr)
         for h in range(2):
@@ -377,9 +388,13 @@
         return pl.pallas_call(
             body,
             out_shape=jax.ShapeDtypeStruct(source.shape, F32),
-            in_specs=[vm] * 3,
+            in_specs=[pl.BlockSpec(memory_space=pl.ANY)] * 3,
             out_specs=vm,
             scratch_shapes=[
+                pltpu.VMEM((2, 2, 2 * H, 2 * H), BF16),
+                pltpu.VMEM((2, 2, 2 * H, 2 * H), BF16),
+                pltpu.VMEM((2, 2, 2 * H, H), BF16),
+                sem((2, 3)),
                 big, big, big, big, big,
                 half, half, half, half,
                 weights, weights, weights, weights, weights,
@@ -390,7 +405,7 @@
                 sem((2, NB)), sem((NB,)), sem((2, NB)), sem((NB,)),
             ],
             compiler_params=pltpu.CompilerParams(
-                collective_id=0, has_side_effects=True, vmem_limit_bytes=48 * 1024 * 1024
+                collective_id=0, has_side_effects=True, vmem_limit_bytes=67043328
             ),
             name="sweep",
         )(ainv, coupling, source)

time: 99.7 us -> 91.9 us (0.922)
  Pallas kernels: 95.6 us -> 89.8 us
  local copies, waits for them, and re-layouts: 3.83 us -> 1.87 us
    pallas_call x1, Pallas kernels: 95.6 us -> 89.8 us  [shards(): pl.pallas_call(body, out_shape=jax.ShapeDtypeStruct(source.shape, F32), i...]
    unnamed x7 -> x1, local copies, waits for them, and re-layouts: 3.83 us -> 1.87 us
where the time goes in v2:
time: 91.9 us; the launch traced here: 91.7 us
  Pallas kernels  89.8 us (98%)
  local copies, waits for them, and re-layouts  1.87 us (2%)
    pallas_call x1, Pallas kernels, shards(): pl.pallas_call(body, out_shape=jax.ShapeDtypeStruct(source.shape, F32), i...  89.8 us
    unnamed x1, local copies, waits for them, and re-layouts  1.87 us

profile of v2, /device:TPU:122, one launch (start us, length us, event | category | flops | bytes accessed | tf_op | source)
XLA Modules:
  0.0 91.7 jit_solution(4773537597005594171)
XLA Ops:
  0.0 89.8 %sweep.1 = f32[1,2,2,256,128]{4,3,2,1,0:T(8,128)} custom-call(bf16[1,2,2,256,256]{4,3,2,1,0:T(8,128)(2,1)} %refs_0_.1, bf16[2,2,256,256]{3,2,1,0:T(8,128)(2,1)} %refs_1_.1, bf16[1,2,2,256,128]{4,3,2,1,0:T(8,128)(2,1)} %refs_2_.1), custom_call_target="tpu_custom_call" | custom-call | tf_op jit(solution)/shard_map/sweep/pallas_call | solution.py:388
  89.8 1.9 %copy.5 = f32[1,2,2,256,128]{4,3,2,1,0:T(8,128)} copy(f32[1,2,2,256,128]{4,3,2,1,0:T(8,128)} %sweep.1) | data formatting | bytes 1048576

commit v3 on v2

v3 whole, which is shorter than its diff:
```python
import jax
import jax.numpy as jnp
from jax import lax
from jax.experimental import pallas as pl
from jax.experimental.pallas import tpu as pltpu
from jax.sharding import PartitionSpec as P

MESH = pl.DeviceIdType.MESH
F32 = jnp.float32
BF16 = jnp.bfloat16

NX = 4
H = 128
R = 16
NA2 = H // R
NA11 = H // 2 // R
NB = H // R
A11_ROW = H
B_ROW = H + H // 2
ROWS = B_ROW + H
A11_CH = NA2
B_CH = NA2 + NA11
NC = B_CH + NB


def dot(a, b):
    return lax.dot_general(a, b, (((1,), (0,)), ((), ())), preferred_element_type=F32)


def split(x):
    hi = x.astype(BF16)
    return hi, (x - hi.astype(F32)).astype(BF16)


def rows(start, size):
    return pl.ds(pl.multiple_of(start, 8), size)


def put_tile(w, t, top):
    w[t, 0:H, :] = top
    w[t, H : 2 * H, 0:H] = -top[:, H:]
    w[t, H : 2 * H, H:] = top[:, :H]


def put_pair(w, t, top):
    hi, lo = split(top)
    put_tile(w.at[0], t, hi)
    put_tile(w.at[1], t, lo)


def unstack(v):
    return jnp.concatenate([v[:, : 2 * H], v[:, 2 * H :]], axis=0)


def stack(y):
    n = y.shape[0] // 2
    return jnp.concatenate([y[:n], y[n:]], axis=1)


def packed(buf):
    return unstack(buf[A11_ROW:B_ROW, :])


def put_weights(w, buf):
    put_pair(w, 0, packed(buf))
    put_pair(w, 1, buf[0:H, 0 : 2 * H])
    put_pair(w, 2, buf[0:H, 2 * H :])


def put_weights_n(w, wb, buf):
    put_pair(w, 0, buf[0:H, 0 : 2 * H])
    put_pair(w, 1, buf[0:H, 2 * H :])
    put_pair(w, 2, packed(buf))
    put_pair(wb, 0, buf[B_ROW:, 0 : 2 * H])
    put_pair(wb, 1, buf[B_ROW:, 2 * H :])


def flip(v):
    return jnp.concatenate([v[:, k : k + H].T for k in range(0, v.shape[1], H)], axis=1)


def turn_a(src, dst, to_plain):
    first, second, third = src[0:H, 0 : 2 * H], src[0:H, 2 * H :], packed(src)
    order = (third, first, second) if to_plain else (second, third, first)
    dst[0:H, 0 : 2 * H] = flip(order[0])
    dst[0:H, 2 * H :] = flip(order[1])
    dst[A11_ROW:B_ROW, :] = stack(flip(order[2]))


def turn_b(src, dst):
    dst[B_ROW:, :] = flip(src[B_ROW:, :])


def mul3(x, w, t):
    n = x.shape[0]
    hi, lo = split(x)
    both = dot(jnp.concatenate([hi, lo], axis=0), w[0, t])
    return both[:n] + both[n:] + dot(hi, w[1, t])


def mul2(x, w, t):
    n = x.shape[0]
    hi, lo = split(x)
    both = dot(jnp.concatenate([hi, lo], axis=0), w[t])
    return both[:n] + both[n:]


def full(x, w, mul):
    x1, x2 = x[:, : 2 * H], x[:, 2 * H :]
    return jnp.concatenate([mul(x1, w, 0) + mul(x2, w, 1), mul(x2, w, 2)], axis=1)


def kernel(
    ndom, nx, nz, ainv_in, coup_in, src_in, out,
    ainv, coup, src, in_sem,
    loc, ez, oz, ex, ox, es, os, nloc, ep, op, ed, od, sd, sx,
    wm, we, wt, wex, wd, wn, wp, wep, wb, wh, inj, fin,
    zs, zr, xs, xr, ss, sr, pr, ds, dr, fs, xds, xdr, zds, zdr,
):
    loads = []
    for s in range(2):
        loads.append([
            pltpu.make_async_copy(ainv_in.at[0, s], ainv.at[s], in_sem.at[s, 0]),
            pltpu.make_async_copy(coup_in.at[s], coup.at[s], in_sem.at[s, 1]),
            pltpu.make_async_copy(src_in.at[0, s], src.at[s], in_sem.at[s, 2]),
        ])
        for load in loads[s]:
            load.start()
    dom, run = lax.axis_index("dom"), lax.axis_index("run")
    x, z = run // nz, run % nz
    y, odd = dom // 2, dom % 2 == 1
    even = jnp.logical_not(odd)
    ny = ndom // 2
    gate = jnp.where(odd, z == 0, z == nz - 1)
    last_x = x == nx - 1
    both = jnp.logical_and

    def at(d, xx, zz):
        return (d, xx * nz + zz)

    z_up, z_dn = at(dom, x, (z + 1) % nz), at(dom, x, (z + nz - 1) % nz)
    x_up, x_dn = at(dom, (x + 1) % nx, z), at(dom, (x + nx - 1) % nx, z)
    d_up, d_dn = at((dom + 2) % ndom, x, z), at((dom + ndom - 2) % ndom, x, z)
    twin = at(dom + 1 - 2 * (dom % 2), x, jnp.where(odd, z + nz - 1, z + 1) % nz)

    barrier = pltpu.get_barrier_semaphore()
    greet = (z_up, z_dn, x_up, x_dn, twin) + ((d_up, d_dn) if ny > 1 else ())
    for who in greet:
        pl.semaphore_signal(barrier, inc=1, device_id=who, device_id_type=MESH)

    for s in range(2):
        for load in loads[s]:
            load.wait()
        ar, ai = ainv[s, 0], ainv[s, 1]
        cr, ci = coup[s, 0], coup[s, 1]
        hr = (dot(ai, ci) - dot(ar, cr)).astype(BF16).astype(F32)
        hi = (-(dot(ar, ci) + dot(ai, cr))).astype(BF16).astype(F32)
        for t, (i, j) in enumerate(((0, 0), (0, H), (H, H))):
            top = jnp.concatenate(
                [hr[i : i + H, j : j + H].T, hi[i : i + H, j : j + H].T], axis=1
            )
            put_tile(wh.at[s], t, top.astype(BF16))
        sr_, si_ = src[s, 0], src[s, 1]
        pr_ = dot(ar, sr_) - dot(ai, si_)
        pi_ = dot(ar, si_) + dot(ai, sr_)
        for h in range(2):
            inj[s, :, 2 * h * H : (2 * h + 1) * H] = pr_[h * H : (h + 1) * H].T
            inj[s, :, (2 * h + 1) * H : (2 * h + 2) * H] = pi_[h * H : (h + 1) * H].T
    w1 = wh.at[1]
    loc[A11_ROW:B_ROW, :] = stack(dot(wh[0, 0, 0:H, :], w1[0]))
    x1, x2 = wh[0, 1, 0:H, :], wh[0, 2, 0:H, :]
    loc[0:H, : 2 * H] = dot(x1, w1[0]) + dot(x2, w1[1])
    loc[0:H, 2 * H :] = dot(x2, w1[2])
    loc[B_ROW:, :] = full(inj[0], w1, mul2) + inj[1]
    put_weights(wm, loc)

    @pl.when(odd)
    def _():
        turn_a(loc, nloc, True)
        turn_b(loc, nloc)
        put_weights_n(wn, wb, nloc)

    pl.semaphore_wait(barrier, len(greet))

    def copy(src_ref, dst_ref, c, ssem, rsem, who, s_off=0):
        return pltpu.make_async_remote_copy(
            src_ref=src_ref.at[rows((c + s_off) * R, R)], dst_ref=dst_ref.at[rows(c * R, R)],
            send_sem=ssem, recv_sem=rsem, device_id=who, device_id_type=MESH,
        )

    def sent(buf, ssem):
        pltpu.make_async_remote_copy(
            src_ref=buf, dst_ref=buf, send_sem=ssem, recv_sem=zr.at[0],
            device_id=z_up, device_id_type=MESH,
        ).wait_send()

    def arrive(buf, rsem, c):
        copy(buf, buf, c, zs, rsem.at[c], z_up).wait_recv()

    def each(lo, hi, body):
        def step(c, carry):
            body(c)
            return carry

        lax.fori_loop(lo, hi, step, 0)

    def when(cond, body):
        pl.when(cond)(body)

    def chain_a(inp, outp, w, rsem, send):
        def a2(c):
            arrive(inp, rsem, c)
            outp[rows(c * R, R), :] = full(inp[rows(c * R, R), :], w, mul3)
            send(c)

        def a11(c):
            arrive(inp, rsem, c)
            outp[rows(c * R, R), :] = stack(mul3(unstack(inp[rows(c * R, R), :]), w, 0))
            send(c)

        each(0, NA2, a2)
        each(A11_CH, B_CH, a11)

    def chain_b(inp, outp, w, own, rsem, send):
        def bb(c):
            arrive(inp, rsem, c)
            r = rows(c * R, R)
            outp[r, :] = full(inp[r, :], w, mul3) + own[r, :]
            send(c)

        each(B_CH, NC, bb)

    def back_a(inp, outp, send):
        def top(c):
            arrive(inp, sr, c)
            v = inp[rows(c * R, R), :]
            v1, v2 = v[:, : 2 * H], v[:, 2 * H :]
            outp[rows(c * R, R), :] = jnp.concatenate(
                [mul3(v1, wn, 0), mul3(v1, wn, 1) + mul3(v2, wn, 2)], axis=1
            )
            send(c)

        def low(c):
            arrive(inp, sr, c)
            outp[rows(c * R, R), :] = stack(mul3(unstack(inp[rows(c * R, R), :]), wn, 2))
            send(c)

        each(0, NA2, top)
        each(A11_CH, B_CH, low)

    def back_b(inp, outp, send):
        def bb(q):
            for half in range(2):
                k = q + half * (NB // 2)
                c = B_CH + k
                arrive(inp, sr, c)
                v = inp[rows(k * R, R), :]
                low = inp[rows(A11_ROW + q * R, R), half * 2 * H : (half + 1) * 2 * H]
                y1 = mul3(v[:, : 2 * H], wb, 0) + mul3(v[:, 2 * H :], wb, 1)
                y2 = mul3(low, wb, 1)
                r = rows(c * R, R)
                outp[r, :] = jnp.concatenate([y1, y2], axis=1) + inp[r, :]
                send(c)

        each(0, NB // 2, bb)

    def z_copy(c, src_ref):
        return copy(src_ref, ez, c, zs, zr.at[c], z_up)

    def s_copy(c, src_ref):
        return copy(src_ref, es, c, ss, sr.at[c], z_dn)

    def x_copy(c, src_ref):
        return copy(src_ref, ex, c, xs, xr.at[c], x_up)

    def p_copy(c):
        return copy(ox, ep, c, xs, pr.at[c], twin)

    def nothing(c):
        pass

    @pl.when(both(even, z == 0))
    def _():
        each(0, NC, lambda c: z_copy(c, loc).start())

    @pl.when(both(even, z > 0))
    def _():
        def send(c):
            when(jnp.logical_not(gate), lambda: z_copy(c, oz).start())
            when(both(gate, x == 0), lambda: x_copy(c, oz).start())

        chain_a(ez, oz, wm, zr, send)
        when(both(gate, x > 0), lambda: put_weights(wt, oz))
        chain_b(ez, oz, wm, loc, zr, send)

    @pl.when(both(odd, z == nz - 1))
    def _():
        each(0, NC, lambda c: s_copy(c, nloc).start())

    @pl.when(both(odd, jnp.logical_and(z > 0, z < nz - 1)))
    def _():
        def send(c):
            s_copy(c, os).start()

        back_a(es, os, send)
        back_b(es, os, send)

    @pl.when(both(odd, z == 0))
    def _():
        def send(c):
            @pl.when(c == 0)
            def _():
                each(0, NC, lambda k: z_copy(k, loc).start())

        back_a(es, os, send)
        turn_a(os, oz, False)
        when(x == 0, lambda: each(0, B_CH, lambda c: x_copy(c, oz).start()))
        when(x > 0, lambda: put_weights(wt, oz))
        back_b(es, os, nothing)
        turn_b(os, oz)
        when(x == 0, lambda: each(B_CH, NC, lambda c: x_copy(c, oz).start()))

    p_all = y > 0

    @pl.when(both(gate, x > 0))
    def _():
        def send(c):
            when(jnp.logical_not(last_x), lambda: x_copy(c, ox).start())
            when(
                both(both(last_x, even), jnp.logical_or(p_all, c >= B_CH)),
                lambda: p_copy(c).start(),
            )

        chain_a(ex, ox, wt, xr, send)
        when(both(last_x, odd), lambda: put_weights(wd, ox))
        chain_b(ex, ox, wt, oz, xr, send)
        put_weights(wex, ex)

    @pl.when(both(odd, z > 0))
    def _():
        @pl.when(z < nz - 1)
        def _():
            def send(c):
                z_copy(c, oz).start()

            chain_a(ez, oz, wm, zr, send)
            chain_b(ez, oz, wm, loc, zr, send)

        when(z == nz - 1, lambda: each(0, NC, lambda c: arrive(ez, zr, c)))

    when(z > 0, lambda: put_weights(we, ez))

    def spread(n, place, buf, ssem, rsem, up, dn):
        plus = (n - 1) // 2

        def up_copy(c):
            return copy(buf, buf, c, ssem.at[0], rsem.at[c], up)

        def dn_copy(c):
            return copy(buf, buf, c, ssem.at[1], rsem.at[c], dn)

        to_up = jnp.logical_or(place == n - 1, place < plus - 1) if plus else place < 0
        to_dn = place > plus

        def go(c):
            when(to_up, lambda: up_copy(c).start())
            when(to_dn, lambda: dn_copy(c).start())

        def drain():
            when(to_up, lambda: sent(buf, ssem.at[0]))
            when(to_dn, lambda: sent(buf, ssem.at[1]))

        return go, drain

    x_go, x_drain = spread(nx, x, sd, xds, xdr, x_up, x_dn)
    z_place = jnp.where(odd, z + nz - 1, z) % nz
    z_go, z_drain = spread(nz, z_place, sx, zds, zdr, z_up, z_dn)

    def first_copy(c):
        return copy(op, ed, c, ds, dr.at[c], d_up, s_off=B_CH)

    def d_copy(c):
        return copy(od, ed, c, ds, dr.at[c], d_up)

    def f_copy(c):
        return copy(ed, sd, c, fs, xdr.at[c], twin)

    head = both(gate, last_x)
    odd_head = both(head, odd)

    @pl.when(odd_head)
    def _():
        if ny > 1:
            @pl.when(both(y > 0, y < ny - 1))
            def _():
                chain_a(ep, op, wd, pr, nothing)
                put_weights(wp, op)

            when(y == ny - 1, lambda: each(0, B_CH, lambda c: arrive(ep, pr, c)))
            when(y > 0, lambda: put_weights(wep, ep))

        def pair(c):
            b = rows(B_ROW + c * R, R)
            arrive(ep, pr, c + B_CH)

            @pl.when(y < ny - 1)
            def _():
                op[b, :] = full(ep[b, :], wd, mul3) + ox[b, :]
                when(y == 0, lambda: first_copy(c).start())

            @pl.when(y == 0)
            def _():
                sd[rows(c * R, R), :] = ep[b, :]
                x_go(c)

        each(0, NB, pair)

        if ny > 1:
            def step(c):
                r, b = rows(c * R, R), rows(B_ROW + c * R, R)
                arrive(ed, dr, c)

                @pl.when(y < ny - 1)
                def _():
                    od[r, :] = full(ed[r, :], wp, mul3) + op[b, :]
                    d_copy(c).start()

                f_copy(c).start()
                sd[r, :] = full(ed[r, :], wep, mul3) + ep[b, :]
                x_go(c)

            when(y > 0, lambda: each(0, NB, step))

    @pl.when(gate)
    def _():
        @pl.when(both(last_x, dom == 0))
        def _():
            sd[...] = jnp.zeros_like(sd)

        def step(c):
            r = rows(c * R, R)

            @pl.when(jnp.logical_not(odd_head))
            def _():
                when(jnp.logical_not(both(last_x, dom == 0)), lambda: arrive(sd, xdr, c))
                x_go(c)

            @pl.when(x == 0)
            def _():
                sx[r, :] = sd[r, :]

            @pl.when(x > 0)
            def _():
                sx[r, :] = full(sd[r, :], wex, mul3) + ex[rows(B_ROW + c * R, R), :]

            z_go(c)

        each(0, NB, step)

    def finish(start, size):
        r = rows(start, size)

        @pl.when(z == 0)
        def _():
            fin[0, r, :] = sx[r, :]

        @pl.when(z > 0)
        def _():
            fin[0, r, :] = full(sx[r, :], we, mul3) + ez[rows(B_ROW + start, size), :]

        s0 = full(fin[0, r, :], wh.at[0], mul2) + inj[0, r, :]
        fin[0, r, :] = s0
        fin[1, r, :] = full(s0, wh.at[1], mul2) + inj[1, r, :]

    @pl.when(jnp.logical_not(gate))
    def _():
        def pass_on(c):
            arrive(sx, zdr, c)
            z_go(c)

        each(0, NB, pass_on)

    each(0, 2, lambda c: finish(c * (H // 2), H // 2))

    for s in range(2):
        for p in range(2):
            for h in range(2):
                k = (2 * h + p) * H
                out[0, s, p, h * H : (h + 1) * H, :] = fin[s, :, k : k + H].T

    when(jnp.logical_or(z == 0, z < nz - 1), lambda: sent(ez, zs))
    when(both(odd, z > 0), lambda: sent(es, ss))
    first_pair = both(both(head, even), jnp.logical_not(p_all))
    when(both(gate, jnp.logical_not(both(last_x, jnp.logical_or(odd, first_pair)))), lambda: sent(ex, xs))
    when(first_pair, lambda: sent(ex.at[B_ROW:ROWS], xs))
    if ny > 1:
        when(both(odd_head, y < ny - 1), lambda: sent(ed, ds))
        when(both(odd_head, y > 0), lambda: sent(ed, fs))
    when(gate, x_drain)
    z_drain()


def build(mesh, nx):
    ndom, nrun = mesh.shape["dom"], mesh.shape["run"]
    nz = nrun // nx

    def shards(ainv, coupling, source):
        big = pltpu.VMEM((ROWS, 4 * H), F32)
        half = pltpu.VMEM((H, 4 * H), F32)
        weights = pltpu.VMEM((2, 3, 2 * H, 2 * H), BF16)
        sem = pltpu.SemaphoreType.DMA

        def body(*refs):
            kernel(ndom, nx, nz, *refs)

        vm = pl.BlockSpec(memory_space=pltpu.VMEM)
        return pl.pallas_call(
            body,
            out_shape=jax.ShapeDtypeStruct(source.shape, F32),
            in_specs=[pl.BlockSpec(memory_space=pltpu.HBM)] * 3,
            out_specs=vm,
            scratch_shapes=[
                pltpu.VMEM((2, 2, 2 * H, 2 * H), BF16),
                pltpu.VMEM((2, 2, 2 * H, 2 * H), BF16),
                pltpu.VMEM((2, 2, 2 * H, H), BF16),
                sem((2, 3)),
                big, big, big, big, big, big, big, big, big, big,
                half, half, half, half,
                weights, weights, weights, weights, weights, weights, weights, weights,
                pltpu.VMEM((2, 2, 2 * H, 2 * H), BF16),
                pltpu.VMEM((2, 3, 2 * H, 2 * H), BF16),
                pltpu.VMEM((2, H, 4 * H), F32),
                pltpu.VMEM((2, H, 4 * H), F32),
                sem, sem((NC,)), sem, sem((NC,)), sem, sem((NC,)), sem((NC,)),
                sem, sem((NB,)), sem,
                sem((2,)), sem((NB,)), sem((2,)), sem((NB,)),
            ],
            compiler_params=pltpu.CompilerParams(
                collective_id=0, has_side_effects=True, vmem_limit_bytes=67043328
            ),
            name="sweep",
        )(ainv, coupling, source)

    in_specs = (
        P(None, ("dom", "run"), None, None, None),
        P(("dom", "run"), None, None, None),
        P(None, ("dom", "run"), None, None, None),
    )
    out_specs = P(None, ("dom", "run"), None, None, None)
    return jax.shard_map(shards, mesh=mesh, in_specs=in_specs, out_specs=out_specs, check_vma=False)


def solution(mesh):
    return build(mesh, NX)
```

time: 91.9 us -> 82.6 us (0.90)
  Pallas kernels: 89.8 us -> 80.6 us
    pallas_call x1, Pallas kernels: 89.8 us -> 80.6 us  [shards(): pl.pallas_call(body, out_shape=jax.ShapeDtypeStruct(source.shape, F32), i...]
where the time goes in v3:
time: 82.6 us; the launch traced here: 82.5 us
  Pallas kernels  80.6 us (98%)
  local copies, waits for them, and re-layouts  1.87 us (2%)
    pallas_call x1, Pallas kernels, shards(): pl.pallas_call(body, out_shape=jax.ShapeDtypeStruct(source.shape, F32), i...  80.6 us
    unnamed x1, local copies, waits for them, and re-layouts  1.87 us

profile of v3, /device:TPU:122, one launch (start us, length us, event | category | flops | bytes accessed | tf_op | source)
XLA Modules:
  0.0 82.5 jit_solution(8876486531548442204)
XLA Ops:
  0.0 80.6 %sweep.1 = f32[1,2,2,256,128]{4,3,2,1,0:T(8,128)} custom-call(bf16[1,2,2,256,256]{4,3,2,1,0:T(8,128)(2,1)} %refs_0_.1, bf16[2,2,256,256]{3,2,1,0:T(8,128)(2,1)} %refs_1_.1, bf16[1,2,2,256,128]{4,3,2,1,0:T(8,128)(2,1)} %refs_2_.1), custom_call_target="tpu_custom_call" | custom-call | tf_op jit(solution)/shard_map/sweep/pallas_call | solution.py:517
  80.6 1.9 %copy.5 = f32[1,2,2,256,128]{4,3,2,1,0:T(8,128)} copy(f32[1,2,2,256,128]{4,3,2,1,0:T(8,128)} %sweep.1) | data formatting | bytes 1048576

commit v4 on v3

--- a/solution.py
+++ b/solution.py
@@ -37,9 +37,14 @@
 
 
 def put_tile(w, t, top):
-    w[t, 0:H, :] = top
-    w[t, H : 2 * H, 0:H] = -top[:, H:]
-    w[t, H : 2 * H, H:] = top[:, :H]
+    k = t * 2 * H
+    w[k : k + H, :] = top
+    w[k + H : k + 2 * H, 0:H] = -top[:, H:]
+    w[k + H : k + 2 * H, H:] = top[:, :H]
+
+
+def tile(t, n=1):
+    return slice(t * 2 * H, (t + n) * 2 * H)
 
 
 def put_pair(w, t, top):
@@ -91,29 +96,28 @@
     dst[B_ROW:, :] = flip(src[B_ROW:, :])
 
 
-def mul3(x, w, t):
+def mul3(x, w, t, k=1):
     n = x.shape[0]
     hi, lo = split(x)
-    both = dot(jnp.concatenate([hi, lo], axis=0), w[0, t])
-    return both[:n] + both[n:] + dot(hi, w[1, t])
-
-
-def mul2(x, w, t):
+    both = dot(jnp.concatenate([hi, lo], axis=0), w[0, tile(t, k), :])
+    return both[:n] + both[n:] + dot(hi, w[1, tile(t, k), :])
+
+
+def mul2(x, w, t, k=1):
     n = x.shape[0]
     hi, lo = split(x)
-    both = dot(jnp.concatenate([hi, lo], axis=0), w[t])
+    both = dot(jnp.concatenate([hi, lo], axis=0), w[tile(t, k), :])
     return both[:n] + both[n:]
 
 
 def full(x, w, mul):
-    x1, x2 = x[:, : 2 * H], x[:, 2 * H :]
-    return jnp.concatenate([mul(x1, w, 0) + mul(x2, w, 1), mul(x2, w, 2)], axis=1)
+    return jnp.concatenate([mul(x, w, 0, 2), mul(x[:, 2 * H :], w, 2)], axis=1)
 
 
 def kernel(
     ndom, nx, nz, ainv_in, coup_in, src_in, out,
     ainv, coup, src, in_sem,
-    loc, ez, oz, ex, ox, es, os, nloc, ep, op, ed, od, sd, sx,
+    loc, ez, oz, ex, ox, es, os, nloc, ep, op, ed, od, o1, sd, sx,
     wm, we, wt, wex, wd, wn, wp, wep, wb, wh, inj, fin,
     zs, zr, xs, xr, ss, sr, pr, ds, dr, fs, xds, xdr, zds, zdr,
 ):
@@ -167,10 +171,10 @@
             inj[s, :, 2 * h * H : (2 * h + 1) * H] = pr_[h * H : (h + 1) * H].T
             inj[s, :, (2 * h + 1) * H : (2 * h + 2) * H] = pi_[h * H : (h + 1) * H].T
     w1 = wh.at[1]
-    loc[A11_ROW:B_ROW, :] = stack(dot(wh[0, 0, 0:H, :], w1[0]))
-    x1, x2 = wh[0, 1, 0:H, :], wh[0, 2, 0:H, :]
-    loc[0:H, : 2 * H] = dot(x1, w1[0]) + dot(x2, w1[1])
-    loc[0:H, 2 * H :] = dot(x2, w1[2])
+    tops = [wh[0, t * 2 * H : t * 2 * H + H, :] for t in range(3)]
+    loc[A11_ROW:B_ROW, :] = stack(dot(tops[0], w1[tile(0), :]))
+    loc[0:H, : 2 * H] = dot(jnp.concatenate([tops[1], tops[2]], axis=1), w1[tile(0, 2), :])
+    loc[0:H, 2 * H :] = dot(tops[2], w1[tile(2), :])
     loc[B_ROW:, :] = full(inj[0], w1, mul2) + inj[1]
     put_weights(wm, loc)
 
@@ -234,9 +238,8 @@
         def top(c):
             arrive(inp, sr, c)
             v = inp[rows(c * R, R), :]
-            v1, v2 = v[:, : 2 * H], v[:, 2 * H :]
             outp[rows(c * R, R), :] = jnp.concatenate(
-                [mul3(v1, wn, 0), mul3(v1, wn, 1) + mul3(v2, wn, 2)], axis=1
+                [mul3(v[:, : 2 * H], wn, 0), mul3(v, wn, 1, 2)], axis=1
             )
             send(c)
 
@@ -256,7 +259,7 @@
                 arrive(inp, sr, c)
                 v = inp[rows(k * R, R), :]
                 low = inp[rows(A11_ROW + q * R, R), half * 2 * H : (half + 1) * 2 * H]
-                y1 = mul3(v[:, : 2 * H], wb, 0) + mul3(v[:, 2 * H :], wb, 1)
+                y1 = mul3(v, wb, 0, 2)
                 y2 = mul3(low, wb, 1)
                 r = rows(c * R, R)
                 outp[r, :] = jnp.concatenate([y1, y2], axis=1) + inp[r, :]
@@ -279,6 +282,14 @@
     def nothing(c):
         pass
 
+    def t_copy(c):
+        return copy(ox, sd, c, fs, xdr.at[c], twin, s_off=B_CH)
+
+    def x_send(c):
+        when(jnp.logical_not(last_x), lambda: x_copy(c, ox).start())
+        when(both(last_x, both(odd, y < ny - 1)), lambda: p_copy(c).start())
+        when(both(both(last_x, dom == 0), c >= B_CH), lambda: t_copy(c - B_CH).start())
+
     @pl.when(both(even, z == 0))
     def _():
         each(0, NC, lambda c: z_copy(c, loc).start())
@@ -291,6 +302,7 @@
 
         chain_a(ez, oz, wm, zr, send)
         when(both(gate, x > 0), lambda: put_weights(wt, oz))
+        when(both(gate, x == 1), lambda: chain_a(ex, ox, wt, xr, x_send))
         chain_b(ez, oz, wm, loc, zr, send)
 
     @pl.when(both(odd, z == nz - 1))
@@ -316,24 +328,16 @@
         turn_a(os, oz, False)
         when(x == 0, lambda: each(0, B_CH, lambda c: x_copy(c, oz).start()))
         when(x > 0, lambda: put_weights(wt, oz))
+        when(x == 1, lambda: chain_a(ex, ox, wt, xr, x_send))
         back_b(es, os, nothing)
         turn_b(os, oz)
         when(x == 0, lambda: each(B_CH, NC, lambda c: x_copy(c, oz).start()))
 
-    p_all = y > 0
-
     @pl.when(both(gate, x > 0))
     def _():
-        def send(c):
-            when(jnp.logical_not(last_x), lambda: x_copy(c, ox).start())
-            when(
-                both(both(last_x, even), jnp.logical_or(p_all, c >= B_CH)),
-                lambda: p_copy(c).start(),
-            )
-
-        chain_a(ex, ox, wt, xr, send)
-        when(both(last_x, odd), lambda: put_weights(wd, ox))
-        chain_b(ex, ox, wt, oz, xr, send)
+        when(x > 1, lambda: chain_a(ex, ox, wt, xr, x_send))
+        when(both(last_x, both(even, y > 0)), lambda: put_weights(wd, ox))
+        chain_b(ex, ox, wt, oz, xr, x_send)
         put_weights(wex, ex)
 
     @pl.when(both(odd, z > 0))
@@ -383,39 +387,34 @@
         return copy(od, ed, c, ds, dr.at[c], d_up)
 
     def f_copy(c):
-        return copy(ed, sd, c, fs, xdr.at[c], twin)
+        return copy(o1, sd, c, fs, xdr.at[c], twin)
 
     head = both(gate, last_x)
-    odd_head = both(head, odd)
-
-    @pl.when(odd_head)
+    even_head = both(head, even)
+
+    @pl.when(even_head)
     def _():
         if ny > 1:
-            @pl.when(both(y > 0, y < ny - 1))
-            def _():
-                chain_a(ep, op, wd, pr, nothing)
-                put_weights(wp, op)
-
-            when(y == ny - 1, lambda: each(0, B_CH, lambda c: arrive(ep, pr, c)))
-            when(y > 0, lambda: put_weights(wep, ep))
-
-        def pair(c):
-            b = rows(B_ROW + c * R, R)
-            arrive(ep, pr, c + B_CH)
-
             @pl.when(y < ny - 1)
             def _():
-                op[b, :] = full(ep[b, :], wd, mul3) + ox[b, :]
-                when(y == 0, lambda: first_copy(c).start())
-
-            @pl.when(y == 0)
-            def _():
-                sd[rows(c * R, R), :] = ep[b, :]
-                x_go(c)
-
-        each(0, NB, pair)
-
-        if ny > 1:
+                each(0, B_CH, lambda c: arrive(ep, pr, c))
+                put_weights(wep, ep)
+
+                @pl.when(y > 0)
+                def _():
+                    for r in (0, H // 2):
+                        op[r : r + H // 2, :] = full(ox[r : r + H // 2, :], wep, mul3)
+                    op[A11_ROW:B_ROW, :] = stack(mul3(packed(ox), wep, 0))
+                    put_weights(wp, op)
+
+                def pair(c):
+                    b = rows(B_ROW + c * R, R)
+                    arrive(ep, pr, c + B_CH)
+                    op[b, :] = full(ox[b, :], wep, mul3) + ep[b, :]
+                    when(y == 0, lambda: first_copy(c).start())
+
+                each(0, NB, pair)
+
             def step(c):
                 r, b = rows(c * R, R), rows(B_ROW + c * R, R)
                 arrive(ed, dr, c)
@@ -425,24 +424,26 @@
                     od[r, :] = full(ed[r, :], wp, mul3) + op[b, :]
                     d_copy(c).start()
 
+                sd[r, :] = ed[r, :]
+                x_go(c)
+                o1[r, :] = full(ed[r, :], wd, mul3) + ox[b, :]
                 f_copy(c).start()
-                sd[r, :] = full(ed[r, :], wep, mul3) + ep[b, :]
-                x_go(c)
 
             when(y > 0, lambda: each(0, NB, step))
 
-    @pl.when(gate)
-    def _():
-        @pl.when(both(last_x, dom == 0))
+        @pl.when(y == 0)
         def _():
             sd[...] = jnp.zeros_like(sd)
-
+            each(0, NB, x_go)
+
+    @pl.when(gate)
+    def _():
         def step(c):
             r = rows(c * R, R)
 
-            @pl.when(jnp.logical_not(odd_head))
+            @pl.when(jnp.logical_not(even_head))
             def _():
-                when(jnp.logical_not(both(last_x, dom == 0)), lambda: arrive(sd, xdr, c))
+                arrive(sd, xdr, c)
                 x_go(c)
 
             @pl.when(x == 0)
@@ -490,12 +491,10 @@
 
     when(jnp.logical_or(z == 0, z < nz - 1), lambda: sent(ez, zs))
     when(both(odd, z > 0), lambda: sent(es, ss))
-    first_pair = both(both(head, even), jnp.logical_not(p_all))
-    when(both(gate, jnp.logical_not(both(last_x, jnp.logical_or(odd, first_pair)))), lambda: sent(ex, xs))
-    when(first_pair, lambda: sent(ex.at[B_ROW:ROWS], xs))
+    when(both(gate, jnp.logical_or(jnp.logical_not(last_x), both(odd, y < ny - 1))), lambda: sent(ex, xs))
+    when(even_head, lambda: sent(sd, fs))
     if ny > 1:
-        when(both(odd_head, y < ny - 1), lambda: sent(ed, ds))
-        when(both(odd_head, y > 0), lambda: sent(ed, fs))
+        when(both(even_head, y < ny - 1), lambda: sent(ed, ds))
     when(gate, x_drain)
     z_drain()
 
@@ -507,7 +506,7 @@
     def shards(ainv, coupling, source):
         big = pltpu.VMEM((ROWS, 4 * H), F32)
         half = pltpu.VMEM((H, 4 * H), F32)
-        weights = pltpu.VMEM((2, 3, 2 * H, 2 * H), BF16)
+        weights = pltpu.VMEM((2, 6 * H, 2 * H), BF16)
         sem = pltpu.SemaphoreType.DMA
 
         def body(*refs):
@@ -525,10 +524,10 @@
                 pltpu.VMEM((2, 2, 2 * H, H), BF16),
                 sem((2, 3)),
                 big, big, big, big, big, big, big, big, big, big,
-                half, half, half, half,
+                half, half, half, half, half,
                 weights, weights, weights, weights, weights, weights, weights, weights,
-                pltpu.VMEM((2, 2, 2 * H, 2 * H), BF16),
-                pltpu.VMEM((2, 3, 2 * H, 2 * H), BF16),
+                pltpu.VMEM((2, 4 * H, 2 * H), BF16),
+                pltpu.VMEM((2, 6 * H, 2 * H), BF16),
                 pltpu.VMEM((2, H, 4 * H), F32),
                 pltpu.VMEM((2, H, 4 * H), F32),
                 sem, sem((NC,)), sem, sem((NC,)), sem, sem((NC,)), sem((NC,)),
@@ -536,10 +535,10 @@
                 sem((2,)), sem((NB,)), sem((2,)), sem((NB,)),
             ],
             compiler_params=pltpu.CompilerParams(
-                collective_id=0, has_side_effects=True, vmem_limit_bytes=67043328
+                collective_id=0, has_side_effects=True, vmem_limit_bytes=48 * 1024 * 1024
             ),
             name="sweep",
-        )(ainv, coupling, source)
+        )(*(pltpu.with_memory_space_constraint(a, pltpu.HBM) for a in (ainv, coupling, source)))
 
     in_specs = (
         P(None, ("dom", "run"), None, None, None),

time: 82.6 us -> 77 us (0.932)
  Pallas kernels: 80.6 us -> 76.1 us
  local copies, waits for them, and re-layouts: 1.87 us -> 0.8 us
    pallas_call x1, Pallas kernels: 80.6 us -> 76.1 us  [shards(): pl.pallas_call(body, out_shape=jax.ShapeDtypeStruct(source.shape, F32), i...]
    unnamed x1, local copies, waits for them, and re-layouts: 1.87 us -> 0.8 us
where the time goes in v4:
time: 77 us; the launch traced here: 76.9 us
  Pallas kernels  76.1 us (99%)
  local copies, waits for them, and re-layouts  0.8 us (1%)
    pallas_call x1, Pallas kernels, shards(): pl.pallas_call(body, out_shape=jax.ShapeDtypeStruct(source.shape, F32), i...  76.1 us

profile of v4, /device:TPU:122, one launch (start us, length us, event | category | flops | bytes accessed | tf_op | source)
XLA Modules:
  0.0 76.9 jit_solution(10239321258624207039)
XLA Ops:
  0.0 76.1 %sweep.1 = f32[1,2,2,256,128]{4,3,2,1,0:T(8,128)S(1)} custom-call(bf16[1,2,2,256,256]{4,3,2,1,0:T(8,128)(2,1)} %refs_0_.1, bf16[2,2,256,256]{3,2,1,0:T(8,128)(2,1)} %refs_1_.1, bf16[1,2,2,256,128]{4,3,2,1,0:T(8,128)(2,1)} %refs_2_.1), custom_call_target="tpu_custom_call" | custom-call | tf_op jit(solution)/shard_map/sweep/pallas_call | solution.py:516
  76.1 0.8 %copy.5 = f32[1,2,2,256,128]{4,3,2,1,0:T(8,128)} copy(f32[1,2,2,256,128]{4,3,2,1,0:T(8,128)S(1)} %sweep.1) | data formatting | bytes 1048576

commit v5 on v4

--- a/solution.py
+++ b/solution.py
@@ -84,12 +84,10 @@
     return jnp.concatenate([v[:, k : k + H].T for k in range(0, v.shape[1], H)], axis=1)
 
 
-def turn_a(src, dst, to_plain):
-    first, second, third = src[0:H, 0 : 2 * H], src[0:H, 2 * H :], packed(src)
-    order = (third, first, second) if to_plain else (second, third, first)
-    dst[0:H, 0 : 2 * H] = flip(order[0])
-    dst[0:H, 2 * H :] = flip(order[1])
-    dst[A11_ROW:B_ROW, :] = stack(flip(order[2]))
+def turn_a(src, dst):
+    dst[0:H, 0 : 2 * H] = flip(packed(src))
+    dst[0:H, 2 * H :] = flip(src[0:H, 0 : 2 * H])
+    dst[A11_ROW:B_ROW, :] = stack(flip(src[0:H, 2 * H :]))
 
 
 def turn_b(src, dst):
@@ -180,7 +178,7 @@
 
     @pl.when(odd)
     def _():
-        turn_a(loc, nloc, True)
+        turn_a(loc, nloc)
         turn_b(loc, nloc)
         put_weights_n(wn, wb, nloc)
 
@@ -222,8 +220,8 @@
             outp[rows(c * R, R), :] = stack(mul3(unstack(inp[rows(c * R, R), :]), w, 0))
             send(c)
 
+        each(A11_CH, B_CH, a11)
         each(0, NA2, a2)
-        each(A11_CH, B_CH, a11)
 
     def chain_b(inp, outp, w, own, rsem, send):
         def bb(c):
@@ -234,7 +232,7 @@
 
         each(B_CH, NC, bb)
 
-    def back_a(inp, outp, send):
+    def back_top(inp, outp, send):
         def top(c):
             arrive(inp, sr, c)
             v = inp[rows(c * R, R), :]
@@ -243,12 +241,14 @@
             )
             send(c)
 
+        each(0, NA2, top)
+
+    def back_low(inp, outp, send):
         def low(c):
             arrive(inp, sr, c)
             outp[rows(c * R, R), :] = stack(mul3(unstack(inp[rows(c * R, R), :]), wn, 2))
             send(c)
 
-        each(0, NA2, top)
         each(A11_CH, B_CH, low)
 
     def back_b(inp, outp, send):
@@ -314,7 +314,8 @@
         def send(c):
             s_copy(c, os).start()
 
-        back_a(es, os, send)
+        back_top(es, os, send)
+        back_low(es, os, send)
         back_b(es, os, send)
 
     @pl.when(both(odd, z == 0))
@@ -324,9 +325,13 @@
             def _():
                 each(0, NC, lambda k: z_copy(k, loc).start())
 
-        back_a(es, os, send)
-        turn_a(os, oz, False)
-        when(x == 0, lambda: each(0, B_CH, lambda c: x_copy(c, oz).start()))
+        back_top(es, os, send)
+        oz[A11_ROW:B_ROW, :] = stack(flip(os[0:H, 0 : 2 * H]))
+        when(x == 0, lambda: each(A11_CH, B_CH, lambda c: x_copy(c, oz).start()))
+        back_low(es, os, send)
+        oz[0:H, 0 : 2 * H] = flip(os[0:H, 2 * H :])
+        oz[0:H, 2 * H :] = flip(packed(os))
+        when(x == 0, lambda: each(0, NA2, lambda c: x_copy(c, oz).start()))
         when(x > 0, lambda: put_weights(wt, oz))
         when(x == 1, lambda: chain_a(ex, ox, wt, xr, x_send))
         back_b(es, os, nothing)
@@ -354,17 +359,15 @@
 
     when(z > 0, lambda: put_weights(we, ez))
 
-    def spread(n, place, buf, ssem, rsem, up, dn):
-        plus = (n - 1) // 2
-
+    def spread(n, place, plus, buf, ssem, rsem, up, dn):
         def up_copy(c):
             return copy(buf, buf, c, ssem.at[0], rsem.at[c], up)
 
         def dn_copy(c):
             return copy(buf, buf, c, ssem.at[1], rsem.at[c], dn)
 
-        to_up = jnp.logical_or(place == n - 1, place < plus - 1) if plus else place < 0
-        to_dn = place > plus
+        to_up = jnp.logical_or(both(place == n - 1, plus > 0), place < plus - 1)
+        to_dn = both(place > plus, plus < n - 1)
 
         def go(c):
             when(to_up, lambda: up_copy(c).start())
@@ -376,9 +379,9 @@
 
         return go, drain
 
-    x_go, x_drain = spread(nx, x, sd, xds, xdr, x_up, x_dn)
+    x_go, x_drain = spread(nx, x, (nx - 1) // 2, sd, xds, xdr, x_up, x_dn)
     z_place = jnp.where(odd, z + nz - 1, z) % nz
-    z_go, z_drain = spread(nz, z_place, sx, zds, zdr, z_up, z_dn)
+    z_go, z_drain = spread(nz, z_place, jnp.where(odd, nz // 2, (nz - 1) // 2), sx, zds, zdr, z_up, z_dn)
 
     def first_copy(c):
         return copy(op, ed, c, ds, dr.at[c], d_up, s_off=B_CH)
@@ -415,21 +418,25 @@
 
                 each(0, NB, pair)
 
-            def step(c):
-                r, b = rows(c * R, R), rows(B_ROW + c * R, R)
-                arrive(ed, dr, c)
-
-                @pl.when(y < ny - 1)
-                def _():
-                    od[r, :] = full(ed[r, :], wp, mul3) + op[b, :]
-                    d_copy(c).start()
-
-                sd[r, :] = ed[r, :]
-                x_go(c)
+            def step(q):
+                for half in range(2):
+                    c = 2 * q + half
+                    r, b = rows(c * R, R), rows(B_ROW + c * R, R)
+                    arrive(ed, dr, c)
+
+                    @pl.when(y < ny - 1)
+                    def _():
+                        od[r, :] = full(ed[r, :], wp, mul3) + op[b, :]
+                        d_copy(c).start()
+
+                    sd[r, :] = ed[r, :]
+                    x_go(c)
+                r, b = rows(2 * q * R, 2 * R), rows(B_ROW + 2 * q * R, 2 * R)
                 o1[r, :] = full(ed[r, :], wd, mul3) + ox[b, :]
-                f_copy(c).start()
-
-            when(y > 0, lambda: each(0, NB, step))
+                for half in range(2):
+                    f_copy(2 * q + half).start()
+
+            when(y > 0, lambda: each(0, NB // 2, step))
 
         @pl.when(y == 0)
         def _():
@@ -479,9 +486,11 @@
             arrive(sx, zdr, c)
             z_go(c)
 
-        each(0, NB, pass_on)
-
-    each(0, 2, lambda c: finish(c * (H // 2), H // 2))
+        for half in range(2):
+            each(half * (NB // 2), (half + 1) * (NB // 2), pass_on)
+            finish(half * (H // 2), H // 2)
+
+    when(gate, lambda: each(0, 2, lambda c: finish(c * (H // 2), H // 2)))
 
     for s in range(2):
         for p in range(2):

time: 77 us -> 78.1 us (1.014)
  Pallas kernels: 76.1 us -> 77.1 us
    pallas_call x1, Pallas kernels: 76.1 us -> 77.1 us  [shards(): pl.pallas_call(body, out_shape=jax.ShapeDtypeStruct(source.shape, F32), i...]
where the time goes in v5:
time: 78.1 us; the launch traced here: 77.9 us
  Pallas kernels  77.1 us (99%)
  local copies, waits for them, and re-layouts  0.8 us (1%)
    pallas_call x1, Pallas kernels, shards(): pl.pallas_call(body, out_shape=jax.ShapeDtypeStruct(source.shape, F32), i...  77.1 us

profile of v5, /device:TPU:122, one launch (start us, length us, event | category | flops | bytes accessed | tf_op | source)
XLA Modules:
  0.0 77.9 jit_solution(11206330927869961222)
XLA Ops:
  0.0 77.1 %sweep.1 = f32[1,2,2,256,128]{4,3,2,1,0:T(8,128)S(1)} custom-call(bf16[1,2,2,256,256]{4,3,2,1,0:T(8,128)(2,1)} %refs_0_.1, bf16[2,2,256,256]{3,2,1,0:T(8,128)(2,1)} %refs_1_.1, bf16[1,2,2,256,128]{4,3,2,1,0:T(8,128)(2,1)} %refs_2_.1), custom_call_target="tpu_custom_call" | custom-call | tf_op jit(solution)/shard_map/sweep/pallas_call | solution.py:525
  77.1 0.8 %copy.5 = f32[1,2,2,256,128]{4,3,2,1,0:T(8,128)} copy(f32[1,2,2,256,128]{4,3,2,1,0:T(8,128)S(1)} %sweep.1) | data formatting | bytes 1048576

commit v6 on v5

--- a/solution.py
+++ b/solution.py
@@ -290,9 +290,15 @@
         when(both(last_x, both(odd, y < ny - 1)), lambda: p_copy(c).start())
         when(both(both(last_x, dom == 0), c >= B_CH), lambda: t_copy(c - B_CH).start())
 
-    @pl.when(both(even, z == 0))
-    def _():
-        each(0, NC, lambda c: z_copy(c, loc).start())
+    def send_own():
+        def own(c):
+            z_copy(c, loc).start()
+
+        each(A11_CH, B_CH, own)
+        each(0, NA2, own)
+        each(B_CH, NC, own)
+
+    when(both(even, z == 0), send_own)
 
     @pl.when(both(even, z > 0))
     def _():
@@ -307,7 +313,12 @@
 
     @pl.when(both(odd, z == nz - 1))
     def _():
-        each(0, NC, lambda c: s_copy(c, nloc).start())
+        def own_b(q):
+            s_copy(B_CH + q, nloc).start()
+            s_copy(B_CH + NB // 2 + q, nloc).start()
+
+        each(0, B_CH, lambda c: s_copy(c, nloc).start())
+        each(0, NB // 2, own_b)
 
     @pl.when(both(odd, jnp.logical_and(z > 0, z < nz - 1)))
     def _():
@@ -321,9 +332,7 @@
     @pl.when(both(odd, z == 0))
     def _():
         def send(c):
-            @pl.when(c == 0)
-            def _():
-                each(0, NC, lambda k: z_copy(k, loc).start())
+            when(c == 0, send_own)
 
         back_top(es, os, send)
         oz[A11_ROW:B_ROW, :] = stack(flip(os[0:H, 0 : 2 * H]))

time: 78.1 us -> 75.4 us (0.965)
  Pallas kernels: 77.1 us -> 74.4 us
    pallas_call x1, Pallas kernels: 77.1 us -> 74.4 us  [shards(): pl.pallas_call(body, out_shape=jax.ShapeDtypeStruct(source.shape, F32), i...]
where the time goes in v6:
time: 75.4 us; the launch traced here: 75.2 us
  Pallas kernels  74.4 us (99%)
  local copies, waits for them, and re-layouts  0.8 us (1%)
    pallas_call x1, Pallas kernels, shards(): pl.pallas_call(body, out_shape=jax.ShapeDtypeStruct(source.shape, F32), i...  74.4 us

profile of v6, /device:TPU:122, one launch (start us, length us, event | category | flops | bytes accessed | tf_op | source)
XLA Modules:
  0.0 75.2 jit_solution(4778677193155395587)
XLA Ops:
  0.0 74.4 %sweep.1 = f32[1,2,2,256,128]{4,3,2,1,0:T(8,128)S(1)} custom-call(bf16[1,2,2,256,256]{4,3,2,1,0:T(8,128)(2,1)} %refs_0_.1, bf16[2,2,256,256]{3,2,1,0:T(8,128)(2,1)} %refs_1_.1, bf16[1,2,2,256,128]{4,3,2,1,0:T(8,128)(2,1)} %refs_2_.1), custom_call_target="tpu_custom_call" | custom-call | tf_op jit(solution)/shard_map/sweep/pallas_call | solution.py:534
  74.4 0.8 %copy.5 = f32[1,2,2,256,128]{4,3,2,1,0:T(8,128)} copy(f32[1,2,2,256,128]{4,3,2,1,0:T(8,128)S(1)} %sweep.1) | data formatting | bytes 1048576

commit v7 on v6

--- a/solution.py
+++ b/solution.py
@@ -174,13 +174,11 @@
     loc[0:H, : 2 * H] = dot(jnp.concatenate([tops[1], tops[2]], axis=1), w1[tile(0, 2), :])
     loc[0:H, 2 * H :] = dot(tops[2], w1[tile(2), :])
     loc[B_ROW:, :] = full(inj[0], w1, mul2) + inj[1]
-    put_weights(wm, loc)
 
     @pl.when(odd)
     def _():
         turn_a(loc, nloc)
         turn_b(loc, nloc)
-        put_weights_n(wn, wb, nloc)
 
     pl.semaphore_wait(barrier, len(greet))
 
@@ -300,6 +298,18 @@
 
     when(both(even, z == 0), send_own)
 
+    @pl.when(both(odd, z == nz - 1))
+    def _():
+        def own_b(q):
+            s_copy(B_CH + q, nloc).start()
+            s_copy(B_CH + NB // 2 + q, nloc).start()
+
+        each(0, B_CH, lambda c: s_copy(c, nloc).start())
+        each(0, NB // 2, own_b)
+
+    put_weights(wm, loc)
+    when(odd, lambda: put_weights_n(wn, wb, nloc))
+
     @pl.when(both(even, z > 0))
     def _():
         def send(c):
@@ -310,15 +320,6 @@
         when(both(gate, x > 0), lambda: put_weights(wt, oz))
         when(both(gate, x == 1), lambda: chain_a(ex, ox, wt, xr, x_send))
         chain_b(ez, oz, wm, loc, zr, send)
-
-    @pl.when(both(odd, z == nz - 1))
-    def _():
-        def own_b(q):
-            s_copy(B_CH + q, nloc).start()
-            s_copy(B_CH + NB // 2 + q, nloc).start()
-
-        each(0, B_CH, lambda c: s_copy(c, nloc).start())
-        each(0, NB // 2, own_b)
 
     @pl.when(both(odd, jnp.logical_and(z > 0, z < nz - 1)))
     def _():
@@ -440,10 +441,18 @@
 
                     sd[r, :] = ed[r, :]
                     x_go(c)
-                r, b = rows(2 * q * R, 2 * R), rows(B_ROW + 2 * q * R, 2 * R)
-                o1[r, :] = full(ed[r, :], wd, mul3) + ox[b, :]
-                for half in range(2):
-                    f_copy(2 * q + half).start()
+
+                    @pl.when(y == ny - 1)
+                    def _():
+                        o1[r, :] = full(ed[r, :], wd, mul3) + ox[b, :]
+                        f_copy(c).start()
+
+                @pl.when(y < ny - 1)
+                def _():
+                    r, b = rows(2 * q * R, 2 * R), rows(B_ROW + 2 * q * R, 2 * R)
+                    o1[r, :] = full(ed[r, :], wd, mul3) + ox[b, :]
+                    for half in range(2):
+                        f_copy(2 * q + half).start()
 
             when(y > 0, lambda: each(0, NB // 2, step))
 
@@ -488,6 +497,9 @@
         s0 = full(fin[0, r, :], wh.at[0], mul2) + inj[0, r, :]
         fin[0, r, :] = s0
         fin[1, r, :] = full(s0, wh.at[1], mul2) + inj[1, r, :]
+
+    when(jnp.logical_or(z == 0, z < nz - 1), lambda: sent(ez, zs))
+    when(both(odd, z > 0), lambda: sent(es, ss))
 
     @pl.when(jnp.logical_not(gate))
     def _():
@@ -507,8 +519,6 @@
                 k = (2 * h + p) * H
                 out[0, s, p, h * H : (h + 1) * H, :] = fin[s, :, k : k + H].T
 
-    when(jnp.logical_or(z == 0, z < nz - 1), lambda: sent(ez, zs))
-    when(both(odd, z > 0), lambda: sent(es, ss))
     when(both(gate, jnp.logical_or(jnp.logical_not(last_x), both(odd, y < ny - 1))), lambda: sent(ex, xs))
     when(even_head, lambda: sent(sd, fs))
     if ny > 1:

time: 75.4 us -> 75.6 us (level)
  no operation moved by 1% of the time
where the time goes in v7:
time: 75.6 us; the launch traced here: 75.5 us
  Pallas kernels  74.7 us (99%)
  local copies, waits for them, and re-layouts  0.8 us (1%)
    pallas_call x1, Pallas kernels, shards(): pl.pallas_call(body, out_shape=jax.ShapeDtypeStruct(source.shape, F32), i...  74.7 us

profile of v7, /device:TPU:122, one launch (start us, length us, event | category | flops | bytes accessed | tf_op | source)
XLA Modules:
  0.0 75.5 jit_solution(15026433434686161902)
XLA Ops:
  0.0 74.7 %sweep.1 = f32[1,2,2,256,128]{4,3,2,1,0:T(8,128)S(1)} custom-call(bf16[1,2,2,256,256]{4,3,2,1,0:T(8,128)(2,1)} %refs_0_.1, bf16[2,2,256,256]{3,2,1,0:T(8,128)(2,1)} %refs_1_.1, bf16[1,2,2,256,128]{4,3,2,1,0:T(8,128)(2,1)} %refs_2_.1), custom_call_target="tpu_custom_call" | custom-call | tf_op jit(solution)/shard_map/sweep/pallas_call | solution.py:544
  74.7 0.8 %copy.5 = f32[1,2,2,256,128]{4,3,2,1,0:T(8,128)} copy(f32[1,2,2,256,128]{4,3,2,1,0:T(8,128)S(1)} %sweep.1) | data formatting | bytes 1048576
